TPU v7x, 128 devices: a whole 4x4x4 slice. The times are simulated.
128 devices in a mesh: ctx: 16 (over z, y_lo, core), ch: 8 (over y_hi, x).
Axes of the slice: x: 4, y: 4 (y_hi: 2, y_lo: 2; y = y_hi * 2 + y_lo), z: 4, core: 2. Of those that a mesh axis runs over, the one named last changes fastest.
Arguments:
- tokens: bfloat16 [2048, 8192], P('ctx', 'ch'), may hold values from -6 to 6
- w_in: bfloat16 [8192, 3, 4096], P('ctx', None, 'ch'), may hold values from -0.0625 to 0.0625
- short_filter: float32 [3, 3, 4096], P(None, None, 'ch'), may hold values from -3 to 3
- decay_rate: float32 [256, 16], P('ch'), may hold values from 0.00024414062 to 0.1
- residue: float32 [256, 16], P('ch'), may hold values from -1.5 to 1.5
- skip: float32 [4096], P('ch'), may hold values from -6 to 6
Outputs:
- block_out: bfloat16 [2048, 4096], P('ctx', 'ch')
All inputs are finite; a program needn't handle non-finite values.
Results may differ from a plain program's by a relative error of at most 0.011.
Values may be sent and summed in bfloat16 or wider, within the bound.
A program may use at most 128 MiB of HBM per device.

v0:
```python
import math
import jax
import jax.numpy as jnp
from jax import lax
from jax.sharding import PartitionSpec as P

GROUP = 16


def shifted(block, axis, distance):
    devices = range(lax.axis_size(axis))
    route = [(i - distance, i) for i in devices if i - distance in devices]
    return lax.ppermute(block, axis, route)


def short_mix(projected, short_filter_taps, block_len, local_width):
    rounded = lax.optimization_barrier(projected.astype(jnp.bfloat16))
    proj_rows = rounded.astype(jnp.float32).reshape(
        block_len + 2, short_filter_taps.shape[1], local_width
    )
    return (
        short_filter_taps[0] * proj_rows[2:]
        + short_filter_taps[1] * proj_rows[1:-1]
        + short_filter_taps[2] * proj_rows[:-2]
    )


def split_parts(weight_full):
    upper_triangle_part = weight_full.astype(jnp.bfloat16)
    lower_triangle_part = (weight_full - upper_triangle_part.astype(jnp.float32)).astype(
        jnp.bfloat16
    )
    return (upper_triangle_part, lower_triangle_part)


def decay_sum(weight_full, input_half_rows):
    upper_triangle_part, lower_triangle_part = split_parts(weight_full)
    first_sum = jnp.einsum(
        "lbu,lvu->lbv", upper_triangle_part, input_half_rows, preferred_element_type=jnp.float32
    )
    second_partial_sum = jnp.einsum(
        "lbu,lvu->lbv", lower_triangle_part, input_half_rows, preferred_element_type=jnp.float32
    )
    return first_sum + second_partial_sum


def local(tokens, w_in, short_filter, decay_rate, residue, skip):
    block_len = tokens.shape[0]
    local_width = w_in.shape[2]
    group_count = local_width // GROUP
    gathered = lax.all_gather(tokens, "ch", axis=1, tiled=True)
    previous = shifted(gathered[block_len - 2 :], "ctx", 1)
    extended = jnp.concatenate([previous, gathered], axis=0)
    shard_piece = lax.all_gather(w_in, "ctx", axis=0, tiled=True)
    flat_piece = shard_piece.reshape(shard_piece.shape[0], -1)
    proj_all = jnp.dot(extended, flat_piece, preferred_element_type=jnp.float32)
    short_mixed = short_mix(proj_all, short_filter, block_len, local_width)
    query_part = short_mixed[:, 0]
    key_part = short_mixed[:, 1]
    value_part = short_mixed[:, 2]
    gated_input = (key_part * value_part).astype(jnp.bfloat16)
    input_t = gated_input.T
    columns_t = input_t.reshape(group_count, GROUP, block_len)
    pole_weight = residue * jnp.sqrt(2.0 * decay_rate)
    positions = jnp.arange(block_len).astype(jnp.float32)
    near_filter = jnp.einsum(
        "gr,grl->gl",
        pole_weight,
        jnp.exp(-decay_rate[:, :, None] * positions[None, None, :]),
        precision=lax.Precision.HIGHEST,
    )
    padded_filter = jnp.concatenate(
        [
            jnp.zeros((group_count, block_len - 1), jnp.float32),
            near_filter,
            jnp.zeros((group_count, 1), jnp.float32),
        ],
        axis=1,
    )

    def near_one(item_pair):
        filter_row, tok_block = item_pair
        span_len = 2 * block_len - 1
        tiled_rows = jnp.tile(filter_row, block_len)[: block_len * span_len].reshape(
            block_len, span_len
        )
        toeplitz = tiled_rows[:, block_len - 1 :]
        upper_triangle_part, lower_triangle_part = split_parts(toeplitz)
        return jnp.dot(
            tok_block, upper_triangle_part, preferred_element_type=jnp.float32
        ) + jnp.dot(tok_block, lower_triangle_part, preferred_element_type=jnp.float32)

    near_field = lax.map(near_one, (padded_filter, columns_t), batch_size=2)
    my_start = lax.axis_index("ctx") * block_len
    empty_state = jnp.zeros((group_count, decay_rate.shape[1], GROUP), jnp.float32)
    shard_piece = lax.all_gather(input_t, "ctx", axis=1, tiled=True)
    piece_len = shard_piece.shape[1]
    sub_len = math.gcd(piece_len, block_len)

    def sub_step(turn_index, carried):
        part_cols = lax.dynamic_slice_in_dim(shard_piece, turn_index * sub_len, sub_len, 1)
        distance = (my_start - 1 - turn_index * sub_len - jnp.arange(sub_len)).astype(jnp.float32)
        decay_factor_weight = jnp.where(
            distance[None, None, :] >= 0.0,
            jnp.exp(-decay_rate[:, :, None] * jnp.maximum(distance, 0.0)[None, None, :]),
            0.0,
        )
        part_input = part_cols.reshape(group_count, GROUP, sub_len)
        return carried + decay_sum(decay_factor_weight, part_input)

    past_state = lax.fori_loop(0, piece_len // sub_len, sub_step, empty_state)
    far_weight = pole_weight[:, :, None] * jnp.exp(
        -decay_rate[:, :, None] * (positions + 1.0)[None, None, :]
    )
    distant_field_output = jnp.einsum(
        "grc,gri->gci", past_state, far_weight, precision=lax.Precision.HIGHEST
    )
    long_out = (near_field + distant_field_output).reshape(local_width, block_len).T
    return (query_part * (long_out + skip * gated_input.astype(jnp.float32))).astype(jnp.bfloat16)


def solution(mesh):
    return jax.shard_map(
        local,
        mesh=mesh,
        in_specs=(
            P("ctx", "ch"),
            P("ctx", None, "ch"),
            P(None, None, "ch"),
            P("ch", None),
            P("ch", None),
            P("ch"),
        ),
        out_specs=P("ctx", "ch"),
        check_vma=False,
    )
```

profile of v0, /device:TPU:1, one launch (start us, length us, event | category | flops | bytes accessed | tf_op | source)
XLA Modules:
  0.0 289.3 jit_solution(2068078018637368503)
XLA Ops:
  7.3 2.6 copy.16
  10.8 55.6 %all-gather.4.cloned.1.call-done = bf16[128,8192]{1,0:T(8,128)(2,1)} async-done(((bf16[128,1024]{1,0:T(8,128)(2,1)}), bf16[128,8192]{1,0:T(8,128)(2,1)}) %all-gather.4.cloned.1.call-update) | async-done | bytes 2097168 | tf_op jit(solution)/shard_map/all_gather | solution.py:51
  66.5 0.9 slice.60
  67.4 4.0 %collective-permute-start = (bf16[2,8192]{1,0:T(2,128)(2,1)S(1)}, bf16[2,8192]{1,0:T(2,128)(2,1)S(1)}, u32[]{:S(2)}, u32[]{:S(2)}) collective-permute-start(bf16[2,8192]{1,0:T(2,128)(2,1)S(1)} %slice.60), channel_id=1, source_target_pairs={{0,8},{8,16},{16,24},{24,32},{32,40},{40,48},{48,56},{56,64},{64,7... | collective-permute-start | bytes 98312 | tf_op jit(solution)/shard_map/ppermute | solution.py:13
  71.6 0.9 collective-permute-done
  72.5 127.4 %all-gather.6.cloned.1.call-done = bf16[8192,3,512]{0,2,1:T(8,128)(2,1)} async-done(((bf16[512,3,512]{0,2,1:T(8,128)(2,1)}), bf16[8192,3,512]{0,2,1:T(8,128)(2,1)}) %all-gather.6.cloned.1.call-update) | async-done | bytes 25165840 | tf_op jit(solution)/shard_map/all_gather | solution.py:54
  199.9 13.7 %convolution_convert_fusion = bf16[130,1536]{1,0:T(8,128)(2,1)S(1)} fusion(bf16[8192,1536]{0,1:T(8,128)(2,1)} %bitcast.89, bf16[128,8192]{1,0:T(8,128)(2,1)} %all-gather.4.cloned.1.call-done, bf16[2,8192]{1,0:T(2,128)(2,1)S(1)} %collective-permute-done), kind=kOutput, calls=%fused_computation.34 | convolution fusion | flops 3276016640 | bytes 27695104 | tf_op jit(solution)/shard_map/dot_general | solution.py:56
  213.8 1.2 copy.19
  217.6 27.3 %while.26 = (s32[]{:T(128)}, f32[16,2,16,128]{3,2,1,0:T(8,128)}, bf16[16,2,16,128]{3,2,1,0:T(8,128)(2,1)S(1)}, f32[16,2,256]{2,1,0:T(2,128)S(1)}, s32[]{:T(128)}) while((s32[]{:T(128)}, f32[16,2,16,128]{3,2,1,0:T(8,128)}, bf16[16,2,16,128]{3,2,1,0:T(8,128)(2,1)S(1)}, f32[16,2,256]{2,1,0:T(2,128)S(1)}, s32[]{:T(128)}) %tuple.71), condition=%wide.region_1.2_spmd, body=%wide.region_0.1_spmd.sunk | while | flops 2232322 | bytes 2100301 | solution.py:93
  225.4 0.8 fusion.60
  228.8 0.8 fusion.60
  232.2 0.8 fusion.60
  233.9 0.8 fusion.60
  235.6 0.8 fusion.60
  245.0 11.1 %all-gather.8.cloned.1.call-done = bf16[512,2048]{1,0:T(8,128)(2,1)} async-done(((bf16[512,128]{1,0:T(8,128)(2,1)}), bf16[512,2048]{1,0:T(8,128)(2,1)}) %all-gather.8.cloned.1.call-update) | async-done | bytes 2097168 | tf_op jit(solution)/shard_map/all_gather | solution.py:96
  256.1 25.0 %while.27 = (s32[]{:T(128)}, f32[32,16,16]{2,1,0:T(8,128)S(1)}, s32[]{:T(128)}, f32[32,16,1]{1,0,2:T(8,128)S(1)}, bf16[512,2048]{1,0:T(8,128)(2,1)}, /*index=5*/s32[]{:T(128)}, s32[]{:T(128)}, s32[]{:T(128)}, s32[]{:T(128)}) while((s32[]{:T(128)}, f32[32,16,16]{2,1,0:T(8,128)S(1)}, s32[]{:T(128)}, f32[32,16,1]{1,0,2:T(8,128)S(1)}, ...), condition=%wide.region_3.4_spmd.clone, body=%wide.region_2.3_spmd.clone.sunk | while | flops 4809480 | bytes 661557 | solution.py:111
  256.1 1.0 constant_dynamic-slice_fusion.2
  257.7 0.9 constant_dynamic-slice_fusion.2
  259.2 0.9 constant_dynamic-slice_fusion.2
  260.8 0.9 constant_dynamic-slice_fusion.2
  262.3 0.9 constant_dynamic-slice_fusion.2
  263.9 0.9 constant_dynamic-slice_fusion.2
  265.5 0.9 constant_dynamic-slice_fusion.2
  267.0 0.9 constant_dynamic-slice_fusion.2
  268.6 0.9 constant_dynamic-slice_fusion.2
  270.1 0.9 constant_dynamic-slice_fusion.2
  271.7 0.9 constant_dynamic-slice_fusion.2
  273.3 0.9 constant_dynamic-slice_fusion.2
  274.8 0.9 constant_dynamic-slice_fusion.2
  276.4 0.9 constant_dynamic-slice_fusion.2
  277.9 0.9 constant_dynamic-slice_fusion.2
  279.5 0.9 constant_dynamic-slice_fusion.2
  (214 shorter events, 38.3 us)
Async XLA Ops:
  6.5 59.9 %all-gather.4.cloned.1.call-start = ((), (), s32[]{:S(2)}) async-start(), calls=%async_computation | async-start | bytes 2359296 | tf_op jit(solution)/shard_map/all_gather | solution.py:51
  7.3 2.8 copy-start.2
  7.3 2.8 copy-start.4
  7.3 3.0 %copy-start.3 = (f32[3,3,512]{2,1,0:T(4,128)S(1)}, f32[3,3,512]{2,1,0:T(4,128)}, u32[]{:S(2)}) copy-start(f32[3,3,512]{2,1,0:T(4,128)} %param.12) | copy-start | bytes 55300
  7.3 192.6 %all-gather.6.cloned.1.call-start = ((), (), s32[]{:S(2)}) async-start(), calls=%async_computation.1 | async-start | bytes 26738688 | tf_op jit(solution)/shard_map/all_gather | solution.py:54
  10.0 246.1 %all-gather.8.cloned.1.call-start = ((), (), s32[]{:S(2)}) async-start(), calls=%async_computation.2 | async-start | bytes 2228224 | tf_op jit(solution)/shard_map/all_gather | solution.py:96
  67.4 5.1 %collective-permute-start = (bf16[2,8192]{1,0:T(2,128)(2,1)S(1)}, bf16[2,8192]{1,0:T(2,128)(2,1)S(1)}, u32[]{:S(2)}, u32[]{:S(2)}) collective-permute-start(bf16[2,8192]{1,0:T(2,128)(2,1)S(1)} %slice.60), channel_id=1, source_target_pairs={{0,8},{8,16},{16,24},{24,32},{32,40},{40,48},{48,56},{56,64},{64,7... | collective-permute-start | bytes 98312 | tf_op jit(solution)/shard_map/ppermute | solution.py:13
  215.0 1.1 copy-start
  256.1 25.0 %copy-start.1 = (f32[16,2,16,128]{3,2,1,0:T(8,128)S(1)}, f32[16,2,16,128]{3,2,1,0:T(8,128)}, u32[]{:S(2)}) copy-start(f32[16,2,16,128]{3,2,1,0:T(8,128)} %get-tuple-element.158) | copy-start | bytes 786436
  256.1 25.8 %copy-start.5 = (f32[512]{0:T(512)S(1)}, f32[512]{0:T(512)}, u32[]{:S(2)}) copy-start(f32[512]{0:T(512)} %param.15) | copy-start | bytes 6148
Sparse Core Ops, SparseCore 0:
  9.7 56.7 all-gather.3
  68.1 131.7 all-gather.5
  217.8 38.2 all-gather.7
where the time goes:
time: 290 us; the launch traced here: 289 us
  waiting for transfers between devices  196 us (68%)
  matrix products  40.5 us (14%)
  local copies, waits for them, and re-layouts  32.3 us (11%)
  between operations  13.3 us (5%)
  starting transfers between devices  4.13 us (1%)
    all_gather x1, waiting for transfers between devices, local(): shard_piece = lax.all_gather(w_in, 'ctx', axis=0, tiled=True)  127 us
    all_gather x1, waiting for transfers between devices, local(): gathered = lax.all_gather(tokens, 'ch', axis=1, tiled=True)  55.6 us
    dynamic_slice x16, local copies, waits for them, and re-layouts, sub_step(): lax.dynamic_slice_in_dim(shard_piece, turn_index * sub_len, sub_len, 1)  14.7 us
    dot_general x1, matrix products, local(): proj_all = jnp.dot(extended, flat_piece, preferred_element_type=jnp.float32)  13.7 us
    dot_general x16, matrix products, near_one(): jnp.dot(tok_block, lower_triangle_part, preferred_element_type=jnp.float32)  13.2 us
    all_gather x1, waiting for transfers between devices, local(): shard_piece = lax.all_gather(input_t, 'ctx', axis=1, tiled=True)  11.1 us
    reshape x16, local copies, waits for them, and re-layouts, near_one(): jnp.tile(filter_row, block_len)[:block_len * span_len]  6.48 us
  transfers between devices with their start and end apart: 4, of which 4 were waited for; matrix products, arithmetic and copies ran while one was open for 11% of the time, Pallas kernels for 0%

commit v1 on v0

--- a/solution.py
+++ b/solution.py
@@ -93,7 +93,9 @@
     near_field = lax.map(near_one, (padded_filter, columns_t), batch_size=2)
     my_start = lax.axis_index("ctx") * block_len
     empty_state = jnp.zeros((group_count, decay_rate.shape[1], GROUP), jnp.float32)
-    shard_piece = lax.all_gather(input_t, "ctx", axis=1, tiled=True)
+    shard_piece = jnp.concatenate(
+        lax.all_to_all(jnp.stack([input_t] * lax.axis_size("ctx")), "ctx", 0, 0), axis=1
+    )
     piece_len = shard_piece.shape[1]
     sub_len = math.gcd(piece_len, block_len)
 

time: 290 us -> 299 us (1.031)
  waiting for transfers between devices: 196 us -> 183 us
  matrix products: 40.5 us -> 51.2 us
  starting transfers between devices: 4.13 us -> 9.18 us
  local copies, waits for them, and re-layouts: 32.3 us -> 36.8 us
    dynamic_slice x16 -> x32, local copies, waits for them, and re-layouts: 14.7 us -> 2.14 us  [sub_step(): lax.dynamic_slice_in_dim(shard_piece, turn_index * sub_len, sub_len, 1)]
    while x32 -> x96, local copies, waits for them, and re-layouts: 3.62 us -> 15.5 us
    all_gather x1 -> x0, waiting for transfers between devices: 11.1 us -> none  [local(): shard_piece = lax.all_gather(input_t, 'ctx', axis=1, tiled=True)]
    dot_general x16, matrix products: 4.81 us -> 14.5 us  [decay_sum(): jnp.einsum('lbu,lvu->lbv', lower_triangle_part, input_half_rows, preferre...]
    all_to_all x0 -> x1, starting transfers between devices: none -> 5.09 us  [local(): lax.all_to_all(jnp.stack([input_t] * lax.axis_size('ctx')), 'ctx', 0, 0)]
  transfers between devices with their start and end apart: 4 -> 4, of which waited for: 4 -> 2; matrix products, arithmetic and copies ran while one was open for 11% -> 11% of each run, Pallas kernels for 0% -> 0%
where the time goes in v1:
time: 299 us; the launch traced here: 298 us
  waiting for transfers between devices  183 us (61%)
  matrix products  51.2 us (17%)
  local copies, waits for them, and re-layouts  36.8 us (12%)
  between operations  13.6 us (5%)
  starting transfers between devices  9.18 us (3%)
    all_gather x1, waiting for transfers between devices, local(): shard_piece = lax.all_gather(w_in, 'ctx', axis=0, tiled=True)  127 us
    all_gather x1, waiting for transfers between devices, local(): gathered = lax.all_gather(tokens, 'ch', axis=1, tiled=True)  55.7 us
    while x96, local copies, waits for them, and re-layouts  15.5 us
    dot_general x16, matrix products, decay_sum(): jnp.einsum('lbu,lvu->lbv', lower_triangle_part, input_half_rows, preferre...  14.5 us
    dot_general x1, matrix products, local(): proj_all = jnp.dot(extended, flat_piece, preferred_element_type=jnp.float32)  13.7 us
    dot_general x16, matrix products, near_one(): jnp.dot(tok_block, lower_triangle_part, preferred_element_type=jnp.float32)  13.2 us
    reshape x16, local copies, waits for them, and re-layouts, near_one(): jnp.tile(filter_row, block_len)[:block_len * span_len]  6.48 us
  transfers between devices with their start and end apart: 4, of which 2 were waited for; matrix products, arithmetic and copies ran while one was open for 11% of the time, Pallas kernels for 0%

profile of v1, /device:TPU:1, one launch (start us, length us, event | category | flops | bytes accessed | tf_op | source)
XLA Modules:
  0.0 298.3 jit_solution(13597870589434384159)
XLA Ops:
  7.3 2.6 copy.32
  10.8 55.7 %all-gather.3.cloned.1.call-done = bf16[128,8192]{1,0:T(8,128)(2,1)} async-done(((bf16[128,1024]{1,0:T(8,128)(2,1)}), bf16[128,8192]{1,0:T(8,128)(2,1)}) %all-gather.3.cloned.1.call-update) | async-done | bytes 2097168 | tf_op jit(solution)/shard_map/all_gather | solution.py:51
  66.5 0.9 slice.60
  67.4 4.0 %collective-permute-start = (bf16[2,8192]{1,0:T(2,128)(2,1)S(1)}, bf16[2,8192]{1,0:T(2,128)(2,1)S(1)}, u32[]{:S(2)}, u32[]{:S(2)}) collective-permute-start(bf16[2,8192]{1,0:T(2,128)(2,1)S(1)} %slice.60), channel_id=1, source_target_pairs={{0,8},{8,16},{16,24},{24,32},{32,40},{40,48},{48,56},{56,64},{64,7... | collective-permute-start | bytes 98312 | tf_op jit(solution)/shard_map/ppermute | solution.py:13
  72.8 127.1 %all-gather.5.cloned.1.call-done = bf16[8192,3,512]{0,2,1:T(8,128)(2,1)} async-done(((bf16[512,3,512]{0,2,1:T(8,128)(2,1)}), bf16[8192,3,512]{0,2,1:T(8,128)(2,1)}) %all-gather.5.cloned.1.call-update) | async-done | bytes 25165840 | tf_op jit(solution)/shard_map/all_gather | solution.py:54
  199.9 13.7 %convolution_convert_fusion = bf16[130,1536]{1,0:T(8,128)(2,1)S(1)} fusion(bf16[8192,1536]{0,1:T(8,128)(2,1)} %bitcast.93, bf16[128,8192]{1,0:T(8,128)(2,1)} %all-gather.3.cloned.1.call-done, bf16[2,8192]{1,0:T(2,128)(2,1)S(1)} %collective-permute-done), kind=kOutput, calls=%fused_computation.34 | convolution fusion | flops 3276016640 | bytes 27695104 | tf_op jit(solution)/shard_map/dot_general | solution.py:56
  213.9 1.2 copy.35
  217.0 1.7 stack.2
  218.7 5.1 %all-to-all-start = ((bf16[16,512,128]{2,1,0:T(8,128)(2,1)}), bf16[16,512,128]{2,1,0:T(8,128)(2,1)}, u32[]{:S(2)}, u32[]{:S(2)}) async-start(bf16[16,512,128]{2,1,0:T(8,128)(2,1)} %stack.2), calls=%async_computation | async-start | bytes 4194304 | tf_op jit(solution)/shard_map/all_to_all | solution.py:97
  223.8 27.3 %while.26 = (s32[]{:T(128)}, f32[16,2,16,128]{3,2,1,0:T(8,128)}, bf16[16,2,16,128]{3,2,1,0:T(8,128)(2,1)S(1)}, f32[16,2,256]{2,1,0:T(2,128)S(1)}, s32[]{:T(128)}) while((s32[]{:T(128)}, f32[16,2,16,128]{3,2,1,0:T(8,128)}, bf16[16,2,16,128]{3,2,1,0:T(8,128)(2,1)S(1)}, f32[16,2,256]{2,1,0:T(2,128)S(1)}, s32[]{:T(128)}) %tuple.70), condition=%wide.region_1.2_spmd, body=%wide.region_0.1_spmd.sunk | while | flops 2232322 | bytes 2100301 | solution.py:93
  238.4 0.8 fusion.60
  240.1 0.8 fusion.60
  241.8 0.8 fusion.60
  251.2 2.9 copy.37
  254.0 34.1 %while.27 = (s32[]{:T(128)}, f32[32,16,16]{2,1,0:T(8,128)S(1)}, s32[]{:T(128)}, f32[32,16,1]{1,0,2:T(8,128)S(1)}, bf16[512,2048]{0,1:T(8,128)(2,1)S(1)}, /*index=5*/s32[]{:T(128)}, s32[]{:T(128)}, s32[]{:T(128)}, s32[]{:T(128)}) while((s32[]{:T(128)}, f32[32,16,16]{2,1,0:T(8,128)S(1)}, s32[]{:T(128)}, f32[32,16,1]{1,0,2:T(8,128)S(1)}, ...), condition=%wide.region_3.4_spmd.clone, body=%wide.region_2.3_spmd.clone.sunk | while | flops 4809480 | bytes 926317 | solution.py:113
  255.2 0.9 fusion.65
  257.4 0.9 fusion.65
  259.5 0.9 fusion.65
  261.6 0.9 fusion.65
  263.8 0.9 fusion.65
  265.9 0.9 fusion.65
  268.0 0.9 fusion.65
  270.2 0.9 fusion.65
  272.3 0.9 fusion.65
  274.4 0.9 fusion.65
  276.6 0.9 fusion.65
  278.7 0.9 fusion.65
  280.8 0.9 fusion.65
  283.0 0.9 fusion.65
  285.1 0.9 fusion.65
  287.2 0.9 fusion.65
  288.1 1.7 convolution_add_fusion.2
  (293 shorter events, 49.5 us)
Async XLA Ops:
  6.5 59.9 %all-gather.3.cloned.1.call-start = ((), (), s32[]{:S(2)}) async-start(), calls=%async_computation.1 | async-start | bytes 2359296 | tf_op jit(solution)/shard_map/all_gather | solution.py:51
  7.3 2.7 copy-start.2
  7.3 2.8 copy-start.6
  7.3 3.0 copy-start.3
  7.3 192.6 %all-gather.5.cloned.1.call-start = ((), (), s32[]{:S(2)}) async-start(), calls=%async_computation.2 | async-start | bytes 26738688 | tf_op jit(solution)/shard_map/all_gather | solution.py:54
  10.3 61.8 %copy-start.1 = (f32[32,16]{1,0:T(8,128)}, f32[32,16]{1,0:T(8,128)S(1)}, u32[]{:S(2)}) copy-start(f32[32,16]{1,0:T(8,128)S(1)} %get-tuple-element.212) | copy-start | bytes 6148
  67.4 5.3 %collective-permute-start = (bf16[2,8192]{1,0:T(2,128)(2,1)S(1)}, bf16[2,8192]{1,0:T(2,128)(2,1)S(1)}, u32[]{:S(2)}, u32[]{:S(2)}) collective-permute-start(bf16[2,8192]{1,0:T(2,128)(2,1)S(1)} %slice.60), channel_id=1, source_target_pairs={{0,8},{8,16},{16,24},{24,32},{32,40},{40,48},{48,56},{56,64},{64,7... | collective-permute-start | bytes 98312 | tf_op jit(solution)/shard_map/ppermute | solution.py:13
  215.0 1.1 copy-start
  218.7 32.4 %all-to-all-start = ((bf16[16,512,128]{2,1,0:T(8,128)(2,1)}), bf16[16,512,128]{2,1,0:T(8,128)(2,1)}, u32[]{:S(2)}, u32[]{:S(2)}) async-start(bf16[16,512,128]{2,1,0:T(8,128)(2,1)} %stack.2), calls=%async_computation | async-start | bytes 4194304 | tf_op jit(solution)/shard_map/all_to_all | solution.py:97
  254.2 0.5 copy-start.4
  254.7 0.5 copy-start.5
  256.9 0.5 copy-start.5
  258.5 0.5 copy-start.4
  259.0 0.5 copy-start.5
  260.6 0.5 copy-start.4
  261.1 0.5 copy-start.5
  262.7 0.5 copy-start.4
  263.2 0.5 copy-start.5
  264.9 0.5 copy-start.4
  265.4 0.5 copy-start.5
  267.5 0.5 copy-start.5
  269.1 0.5 copy-start.4
  269.6 0.5 copy-start.5
  271.3 0.5 copy-start.4
  271.8 0.5 copy-start.5
  273.9 0.5 copy-start.5
  276.0 0.5 copy-start.5
  278.2 0.5 copy-start.5
  280.3 0.5 copy-start.5
  282.4 0.5 copy-start.5
  284.6 0.5 copy-start.5
  286.7 0.5 copy-start.5
  (9 other events, 4.6 us)
Sparse Core Ops, SparseCore 0:
  9.7 56.7 all-gather.2
  68.1 131.6 all-gather.4
